TPU v7x, 32 devices: a whole 2x2x4 slice. The times are simulated.
32 devices in a mesh: item: 16 (over z, x, core), grp: 2 (over y).
Axes of the slice: x: 2, y: 2, z: 4, core: 2. Of those that a mesh axis runs over, the one named last changes fastest.
Arguments:
- hidden: bfloat16 [768, 256], P(('grp', 'item')), may hold values from -400 to 400
- item_table: bfloat16 [131072, 256], P('item'), may hold values from -1.5 to 1.5
- targets: int32 [768], P(('grp', 'item')), may hold values from 0 to 131071
- lengths: int32 [2, 16], replicated, may hold values from 1 to 96, 384 in all within a row
Outputs:
- row_loss: float32 [768], P(('grp', 'item'))
- hidden_grad: bfloat16 [768, 256], P(('grp', 'item'))
- table_grad: bfloat16 [131072, 256], P(('item', 'grp'))
Inputs may be any that keep to these rules, and one draw needn't show every extreme that they name: Each row holds the lengths of the 16 user sequences that fill one group's 384 positions in order, and sums to 384.
All inputs are finite; a program needn't handle non-finite values.
Results may differ from a plain program's by a relative error of at most 0.0047.
Values may be sent and summed in bfloat16 or wider, within the bound.
A program may use at most 64 MiB of HBM per device.

v0:
```python
import jax
import jax.numpy as jnp
from jax import lax
from jax.sharding import PartitionSpec as P


def block_width():
    return 2048


def weights_for(lengths, group_index, group_rows):
    seq_count = lengths.shape[1]
    own_lengths = lax.dynamic_index_in_dim(lengths, group_index, 0, keepdims=False)
    seq_ends = jnp.cumsum(own_lengths)
    starts = seq_ends - own_lengths
    places = jnp.arange(group_rows, dtype=jnp.int32)
    inside = (places[:, None] >= starts[None, :]) & (places[:, None] < seq_ends[None, :])
    row_length = jnp.sum(
        jnp.where(inside, own_lengths[None, :].astype(jnp.float32), jnp.float32(0.0)), axis=1
    )
    return group_rows / seq_count / row_length


def split_blocks(item_table, first_item, block_size):
    block_count = item_table.shape[0] // block_size
    blocks = item_table.reshape(block_count, block_size, item_table.shape[1])
    block_starts = first_item + block_size * jnp.arange(block_count, dtype=jnp.int32)
    return (blocks, block_starts)


def partial_stats(states, target_ids, item_table, first_item, block_size):
    blocks, block_starts = split_blocks(item_table, first_item, block_size)
    row_count = states.shape[0]

    def partial_visit(carried, block_pair):
        highest, running, picked = carried
        item_block, block_start = block_pair
        scores = jnp.einsum("rd,id->ri", states, item_block, preferred_element_type=jnp.float32)
        new_max = jnp.maximum(highest, jnp.max(scores, axis=1))
        running = running * jnp.exp(highest - new_max) + jnp.sum(
            jnp.exp(scores - new_max[:, None]), axis=1
        )
        columns = block_start + jnp.arange(block_size, dtype=jnp.int32)
        matched = target_ids[:, None] == columns[None, :]
        picked = picked + jnp.sum(jnp.where(matched, scores, jnp.float32(0.0)), axis=1)
        return ((new_max, running, picked), None)

    start_stats = (
        jnp.full((row_count,), -jnp.inf, dtype=jnp.float32),
        jnp.zeros((row_count,), jnp.float32),
        jnp.zeros((row_count,), jnp.float32),
    )
    final_stats, unused = lax.scan(partial_visit, start_stats, (blocks, block_starts))
    return final_stats


def backward(states, target_ids, item_table, first_item, block_size, log_total, row_weight):
    blocks, block_starts = split_blocks(item_table, first_item, block_size)

    def backward_visit(state_grad, block_pair):
        item_block, block_start = block_pair
        scores = jnp.einsum("rd,id->ri", states, item_block, preferred_element_type=jnp.float32)
        columns = block_start + jnp.arange(block_size, dtype=jnp.int32)
        matched = (target_ids[:, None] == columns[None, :]).astype(jnp.float32)
        signal = (row_weight[:, None] * (jnp.exp(scores - log_total[:, None]) - matched)).astype(
            jnp.bfloat16
        )
        state_grad = state_grad + jnp.dot(signal, item_block, preferred_element_type=jnp.float32)
        item_grad = jnp.einsum("ri,rd->id", signal, states, preferred_element_type=jnp.float32)
        return (state_grad, item_grad)

    start_grad = jnp.zeros((states.shape[0], states.shape[1]), jnp.float32)
    state_grad, item_grads = lax.scan(backward_visit, start_grad, (blocks, block_starts))
    return (state_grad, item_grads.reshape(item_table.shape[0], item_table.shape[1]))


def local(hidden, item_table, targets, lengths):
    rows_local = hidden.shape[0]
    items_local = item_table.shape[0]
    block_size = block_width()
    item_rank = lax.axis_index("item")
    group_rank = lax.axis_index("grp")
    first_item = item_rank * items_local
    group_states, group_targets = (
        lax.all_gather(hidden, "item", axis=0, tiled=True),
        lax.all_gather(targets, "item", axis=0, tiled=True),
    )
    group_rows = group_states.shape[0]
    states, target_ids = (
        lax.all_gather(group_states, "grp", axis=0, tiled=True),
        lax.all_gather(group_targets, "grp", axis=0, tiled=True),
    )
    row_weight = jnp.concatenate(
        [weights_for(lengths, member, group_rows) for member in range(lengths.shape[0])]
    )
    own_start = group_rank * group_rows + item_rank * rows_local
    highest, running, picked = partial_stats(states, target_ids, item_table, first_item, block_size)
    row_max = lax.pmax(highest, "item")
    exp_total, target_score = lax.psum((running * jnp.exp(highest - row_max), picked), "item")
    log_total = row_max + jnp.log(exp_total)
    losses = log_total - target_score
    row_loss = lax.dynamic_slice_in_dim(losses, own_start, rows_local)
    half_items = items_local // 2
    own_items = lax.dynamic_slice_in_dim(item_table, group_rank * half_items, half_items)
    state_grad, table_grad = backward(
        states,
        target_ids,
        own_items,
        first_item + group_rank * half_items,
        block_width(),
        log_total,
        row_weight,
    )
    group_grad = lax.psum_scatter(state_grad, "grp", scatter_dimension=0, tiled=True)
    hidden_grad = lax.psum_scatter(group_grad, "item", scatter_dimension=0, tiled=True)
    return (row_loss, hidden_grad.astype(jnp.bfloat16), table_grad.astype(jnp.bfloat16))


def solution(mesh):
    in_specs = (P(("grp", "item"), None), P("item", None), P(("grp", "item")), P())
    out_specs = (P(("grp", "item")), P(("grp", "item"), None), P(("item", "grp"), None))
    return jax.shard_map(local, mesh=mesh, in_specs=in_specs, out_specs=out_specs, check_vma=False)
```

profile of v0, /device:TPU:1, one launch (start us, length us, event | category | flops | bytes accessed | tf_op | source)
XLA Modules:
  0.0 233.8 jit_solution(2730930800067419069)
XLA Ops:
  10.8 10.7 %all-reduce = s32[384]{0:T(512)S(1)} all-reduce(s32[384]{0:T(512)S(1)} %dynamic-update-slice), channel_id=1, replica_groups=mesh['item'=16,'grp'=2] {'item'}, use_global_device_ids=true, to_apply=%add | all-reduce | flops 384 | bytes 3072
  21.5 3.2 %all-gather = s32[2,1,384]{2,1,0:T(1,128)S(1)} all-gather(s32[1,1,384]{2,1,0:T(1,128)S(1)} %reshape.56), channel_id=1, replica_groups=mesh['item'=16,'grp'=2] {'grp'}, dimensions={0}, use_global_device_ids=true | all-gather | bytes 4608 | tf_op jit(solution)/shard_map/all_gather | solution.py:91
  26.1 22.8 %all_gather.12 = bf16[384,256]{1,0:T(8,128)(2,1)S(1)} all-gather(bf16[24,256]{1,0:T(8,128)(2,1)} %param.8), channel_id=1, replica_groups=mesh['item'=16,'grp'=2] {'item'}, dimensions={0}, use_global_device_ids=true | all-gather | bytes 208896 | tf_op jit(solution)/shard_map/all_gather | solution.py:85
  48.9 6.9 %all_gather.13 = bf16[768,256]{1,0:T(8,128)(2,1)S(1)} all-gather(bf16[384,256]{1,0:T(8,128)(2,1)S(1)} %all_gather.12), channel_id=1, replica_groups=mesh['item'=16,'grp'=2] {'grp'}, dimensions={0}, use_global_device_ids=true | all-gather | bytes 589824 | tf_op jit(solution)/shard_map/all_gather | solution.py:90
  55.8 20.3 %while.28 = (s32[]{:T(128)}, f32[768]{0:T(1024)S(1)}, f32[768]{0:T(1024)S(1)}, f32[768]{0:T(1024)S(1)}, bf16[4,2048,256]{2,1,0:T(8,128)(2,1)}, /*index=5*/bf16[7...) while((s32[]{:T(128)}, f32[768]{0:T(1024)S(1)}, ...), condition=%wide.region_4.5_spmd.clone, body=%wide.region_0.4_spmd.clone.sunk | while | flops 814750208 | bytes 14096524 | solution.py:53
  57.1 2.3 fusion.40
  59.3 1.5 fusion.41
  62.1 2.3 fusion.40
  64.4 1.5 fusion.41
  67.2 2.3 fusion.40
  69.5 1.5 fusion.41
  72.3 2.3 fusion.40
  74.6 1.5 fusion.41
  76.1 29.9 %pmax.7 = f32[768]{0:T(1024)S(1)} all-reduce(f32[768]{0:T(1024)S(1)} %get-tuple-element.95), channel_id=1, replica_groups=mesh['item'=16,'grp'=2] {'item'}, use_global_device_ids=true, to_apply=%region_5.6 | all-reduce | flops 768 | bytes 6144 | tf_op jit(solution)/shard_map/pmax | solution.py:98
  106.0 1.7 constant_dynamic-slice_fusion
  107.8 30.3 %all-reduce.1 = (f32[768]{0:T(1024)S(1)}, f32[768]{0:T(1024)S(1)}) all-reduce(f32[768]{0:T(1024)S(1)} %exponential_multiply_fusion, f32[768]{0:T(1024)S(1)} %get-tuple-element.97), channel_id=1, replica_groups=mesh['item'=16,'grp'=2] {'item'}, use_global_device_ids=true, to_apply=%region_6.7 | all-reduce | flops 1536 | bytes 12288 | tf_op jit(solution)/shard_map/psum | solution.py:99
  138.1 14.3 %while.29 = (s32[]{:T(128)}, f32[768,256]{1,0:T(8,128)S(1)}, bf16[2,2048,256]{2,1,0:T(8,128)(2,1)}, f32[768]{0:T(1024)S(1)}, bf16[2,2048,256]{2,1,0:T(8,128)(2,1...) while((s32[]{:T(128)}, f32[768,256]{1,0:T(8,128)S(1)}, ...), condition=%wide.region_13.14_spmd.clone, body=%wide.region_12.13_spmd.clone.sunk | while | flops 2425751552 | bytes 32796884 | solution.py:73
  139.3 1.9 fusion.48
  143.9 1.3 copy-done.2
  146.4 1.9 fusion.48
  151.0 1.3 copy-done.2
  153.3 14.7 %reduce-scatter.3.cloned.1.call-done = f32[384,256]{1,0:T(8,128)} async-done(((f32[768,256]{1,0:T(8,128)}), f32[384,256]{1,0:T(8,128)}) %reduce-scatter.3.cloned.1.call-update) | async-done | bytes 393232 | tf_op jit(solution)/shard_map/reduce_scatter | solution.py:114
  168.6 57.0 %reduce-scatter.5.cloned.1.call-done = f32[24,256]{1,0:T(8,128)} async-done(((f32[384,256]{1,0:T(8,128)}), f32[24,256]{1,0:T(8,128)}) %reduce-scatter.5.cloned.1.call-update) | async-done | bytes 24592 | tf_op jit(solution)/shard_map/reduce_scatter | solution.py:115
  225.6 1.3 convert_element_type.23
  (68 shorter events, 18.5 us)
Async XLA Ops:
  7.2 160.8 %reduce-scatter.3.cloned.1.call-start = ((), (), s32[]{:S(2)}) async-start(), calls=%async_computation.2 | async-start | bytes 1179648 | tf_op jit(solution)/shard_map/reduce_scatter | solution.py:114
  141.3 1.6 copy-start.1
  143.9 1.3 copy-start.2
  148.4 1.6 copy-start.1
  151.0 1.3 copy-start.2
  152.3 0.9 copy-start
  153.2 72.4 %reduce-scatter.5.cloned.1.call-start = ((), (), s32[]{:S(2)}) async-start(), calls=%async_computation.3 | async-start | bytes 417792 | tf_op jit(solution)/shard_map/reduce_scatter | solution.py:115
Sparse Core Ops, SparseCore 0:
  153.4 14.5 reduce-scatter.2
  171.5 54.1 reduce-scatter.4
where the time goes:
time: 237 us; the launch traced here: 234 us
  blocking collectives  104 us (44%)
  waiting for transfers between devices  71.7 us (30%)
  matrix products  17.4 us (7%)
  between operations  14.8 us (6%)
  local copies, waits for them, and re-layouts  13.1 us (6%)
  other arithmetic  12.6 us (5%)
    reduce_scatter x1, waiting for transfers between devices, local(): lax.psum_scatter(group_grad, 'item', scatter_dimension=0, tiled=True)  57 us
    psum x1, blocking collectives, local(): lax.psum((running * jnp.exp(highest - row_max), picked), 'item')  30.3 us
    pmax x1, blocking collectives, local(): row_max = lax.pmax(highest, 'item')  29.9 us
    all_gather x1, blocking collectives, local(): lax.all_gather(hidden, 'item', axis=0, tiled=True)  22.8 us
    reduce_scatter x1, waiting for transfers between devices, local(): lax.psum_scatter(state_grad, 'grp', scatter_dimension=0, tiled=True)  14.7 us
    unnamed x1, blocking collectives  10.7 us
    dot_general x4, matrix products, partial_visit(): jnp.einsum('rd,id->ri', states, item_block, preferred_element_type=jnp.fl...  9.01 us
    all_gather x1, blocking collectives, local(): lax.all_gather(group_states, 'grp', axis=0, tiled=True)  6.94 us
  transfers between devices with their start and end apart: 2, of which 2 were waited for; matrix products, arithmetic and copies ran while one was open for 0% of the time, Pallas kernels for 0%

commit v1 on v0

--- a/solution.py
+++ b/solution.py
@@ -1,6 +1,9 @@
+import functools
 import jax
 import jax.numpy as jnp
 from jax import lax
+from jax.experimental import pallas as pl
+from jax.experimental.pallas import tpu as pltpu
 from jax.sharding import PartitionSpec as P
 
 
@@ -116,7 +119,492 @@
     return (row_loss, hidden_grad.astype(jnp.bfloat16), table_grad.astype(jnp.bfloat16))
 
 
+def fused_kernel(
+    item_size,
+    group_size,
+    chunk,
+    hidden_ref,
+    targets_ref,
+    lengths_ref,
+    table_ref,
+    loss_ref,
+    hgrad_ref,
+    tgrad_ref,
+    target_pad,
+    gathered,
+    states,
+    items,
+    items_t,
+    probs,
+    signal,
+    chunk_max,
+    own_stats,
+    mate_stats,
+    all_stats,
+    grad_t,
+    grads,
+    mate_grads,
+    send_grads,
+    recv_grads,
+    stage,
+    items_sem,
+    out_sems,
+    gather_send,
+    gather_recv,
+    relay_send,
+    relay_recv,
+    stat_mate_sems,
+    stat_send,
+    stat_recv,
+    grad_mate_sems,
+    grad_send,
+    grad_recv,
+):
+    rows, width = hidden_ref.shape
+    half = items.shape[0]
+    chunk_count = half // chunk
+    padded = gathered.shape[1]
+    positions = states.shape[0]
+    chips_per_group = item_size // 2
+    chips = chips_per_group * group_size
+    group_rows = rows * item_size
+
+    item_rank = lax.axis_index("item")
+    group_rank = lax.axis_index("grp")
+    core = lax.rem(item_rank, 2)
+    chip = group_rank * chips_per_group + item_rank // 2
+    own_block = group_rank * item_size + item_rank
+    first_item = (item_rank * group_size + group_rank) * half
+
+    def chip_device(which, core_index):
+        return {
+            "item": 2 * lax.rem(which, chips_per_group) + core_index,
+            "grp": which // chips_per_group,
+        }
+
+    def block_of(which, core_index):
+        return (
+            (which // chips_per_group) * item_size
+            + 2 * lax.rem(which, chips_per_group)
+            + core_index
+        )
+
+    mate = {"item": 2 * (item_rank // 2) + 1 - core, "grp": group_rank}
+
+    def remote(src, dst, send_sem, recv_sem, device):
+        return pltpu.make_async_remote_copy(
+            src_ref=src,
+            dst_ref=dst,
+            send_sem=send_sem,
+            recv_sem=recv_sem,
+            device_id=device,
+            device_id_type=pl.DeviceIdType.MESH,
+        )
+
+    def each_peer(body):
+        def step(offset, carried):
+            body(lax.rem(chip + offset, chips))
+            return carried
+
+        lax.fori_loop(1, chips, step, 0)
+
+    def each_source(body):
+        def step(offset, carried):
+            body(lax.rem(chip + chips - offset, chips))
+            return carried
+
+        lax.fori_loop(1, chips, step, 0)
+
+    items_copy = pltpu.make_async_copy(
+        table_ref.at[pl.ds(pl.multiple_of(group_rank * half, chunk), half)], items, items_sem
+    )
+    items_copy.start()
+
+    barrier = pltpu.get_barrier_semaphore()
+    pl.semaphore_signal(barrier, inc=1, device_id=mate, device_id_type=pl.DeviceIdType.MESH)
+    each_peer(
+        lambda peer: pl.semaphore_signal(
+            barrier,
+            inc=1,
+            device_id=chip_device(peer, core),
+            device_id_type=pl.DeviceIdType.MESH,
+        )
+    )
+
+    target_pad[...] = jnp.zeros_like(target_pad)
+    target_pad[0:1, 0:rows] = targets_ref[...]
+    wide_targets = jnp.broadcast_to(target_pad[0:1, :], (8, width))
+    digit_row = lax.broadcasted_iota(jnp.int32, (8, width), 0)
+    digits = jnp.where(
+        digit_row == 0,
+        wide_targets & 255,
+        jnp.where(
+            digit_row == 1,
+            (wide_targets >> 8) & 255,
+            jnp.where(digit_row == 2, (wide_targets >> 16) & 255, 0),
+        ),
+    ).astype(jnp.float32)
+    gathered[own_block] = jnp.concatenate(
+        [hidden_ref[...].astype(jnp.float32), digits], axis=0
+    ).astype(jnp.bfloat16)
+
+    pl.semaphore_wait(barrier, chips)
+
+    def gather_copy(peer):
+        return remote(
+            gathered.at[own_block],
+            gathered.at[own_block],
+            gather_send.at[peer],
+            gather_recv.at[chip],
+            chip_device(peer, core),
+        )
+
+    def gather_arrival(source):
+        block = gathered.at[block_of(source, core)]
+        return remote(
+            block, block, gather_send.at[source], gather_recv.at[source], chip_device(source, core)
+        )
+
+    def relay_copy(source):
+        block = gathered.at[block_of(source, core)]
+        return remote(block, block, relay_send.at[source], relay_recv.at[source], mate)
+
+    def relay_arrival(source):
+        block = gathered.at[block_of(source, 1 - core)]
+        return remote(block, block, relay_send.at[source], relay_recv.at[source], mate)
+
+    each_peer(lambda peer: gather_copy(peer).start())
+    relay_copy(chip).start()
+
+    places = lax.broadcasted_iota(jnp.int32, (1, positions), 1)
+    row_length = jnp.zeros((1, positions), jnp.float32)
+    for member in range(group_size):
+        start = member * group_rows
+        for seq in range(lengths_ref.shape[1]):
+            length = lengths_ref[member, seq]
+            inside = (places >= start) & (places < start + length)
+            row_length = jnp.where(inside, length.astype(jnp.float32), row_length)
+            start = start + length
+    weight = (group_rows / lengths_ref.shape[1]) / row_length
+
+    items_copy.wait()
+    for index in range(chunk_count):
+        span = pl.ds(index * chunk, chunk)
+        items_t[:, span] = items[span, :].astype(jnp.float32).T.astype(jnp.bfloat16)
+
+    def pass_on(source):
+        gather_arrival(source).wait_recv()
+        relay_copy(source).start()
+
+    each_source(pass_on)
+    relay_arrival(chip).wait_recv()
+    each_source(lambda source: relay_arrival(source).wait_recv())
+
+    everything = gathered[...].astype(jnp.float32)
+    states[...] = everything[:, :rows, :].reshape(positions, width).astype(jnp.bfloat16)
+    lanes = 128
+    code = everything[:, rows:padded, :lanes]
+    code_rows = code.shape[0] * code.shape[1]
+    code = code.reshape(code_rows, lanes).astype(jnp.bfloat16)
+    lane_index = lax.broadcasted_iota(jnp.int32, (lanes, positions), 0)
+    place_index = lax.broadcasted_iota(jnp.int32, (lanes, positions), 1)
+    spread = (lax.rem(place_index, rows) == lane_index).astype(jnp.float32).astype(jnp.bfloat16)
+    coded = jnp.dot(code, spread, preferred_element_type=jnp.float32)
+    code_index = lax.broadcasted_iota(jnp.int32, (code_rows, positions), 0)
+    code_place = lax.broadcasted_iota(jnp.int32, (code_rows, positions), 1)
+    digit = lax.rem(code_index, 8)
+    scale = jnp.where(
+        digit == 0,
+        jnp.float32(1.0),
+        jnp.where(
+            digit == 1,
+            jnp.float32(256.0),
+            jnp.where(digit == 2, jnp.float32(65536.0), jnp.float32(0.0)),
+        ),
+    )
+    target_ids = jnp.sum(
+        jnp.where(code_index // 8 == code_place // rows, coded * scale, 0.0),
+        axis=0,
+        keepdims=True,
+    ).astype(jnp.int32)
+    local_target = target_ids - first_item
+
+    def forward(index, carried):
+        highest, running, picked = carried
+        base = pl.multiple_of(index * chunk, chunk)
+        scores = lax.dot_general(
+            items[pl.ds(base, chunk), :],
+            states[...],
+            (((1,), (1,)), ((), ())),
+            preferred_element_type=jnp.float32,
+        )
+        top = jnp.max(scores, axis=0, keepdims=True)
+        exps = jnp.exp(scores - top)
+        probs[pl.ds(base, chunk), :] = exps
+        chunk_max[index] = top
+        total = jnp.sum(exps, axis=0, keepdims=True)
+        item_index = lax.broadcasted_iota(jnp.int32, (chunk, positions), 0)
+        matched = item_index == local_target - base
+        picked = picked + jnp.sum(jnp.where(matched, scores, 0.0), axis=0, keepdims=True)
+        new_max = jnp.maximum(highest, top)
+        running = running * jnp.exp(highest - new_max) + total * jnp.exp(top - new_max)
+        return (new_max, running, picked)
+
+    zero_row = jnp.zeros((1, positions), jnp.float32)
+    highest, running, picked = lax.fori_loop(
+        0,
+        chunk_count,
+        forward,
+        (jnp.full((1, positions), -jnp.inf, jnp.float32), zero_row, zero_row),
+    )
+    own_stats[0:1, :] = highest + jnp.log(running)
+    own_stats[1:2, :] = picked
+
+    stat_mate = remote(
+        own_stats, mate_stats, stat_mate_sems.at[0], stat_mate_sems.at[1], mate
+    )
+    stat_mate.start()
+    stat_mate.wait()
+
+    def log_add(a, b):
+        top = jnp.maximum(a, b)
+        return top + jnp.log(jnp.exp(a - top) + jnp.exp(b - top))
+
+    all_stats[chip] = jnp.concatenate(
+        [
+            log_add(own_stats[0:1, :], mate_stats[0:1, :]),
+            own_stats[1:2, :] + mate_stats[1:2, :],
+        ],
+        axis=0,
+    )
+
+    def stat_copy(peer):
+        return remote(
+            all_stats.at[chip],
+            all_stats.at[chip],
+            stat_send.at[peer],
+            stat_recv.at[chip],
+            chip_device(peer, core),
+        )
+
+    def stat_arrival(source):
+        return remote(
+            all_stats.at[source],
+            all_stats.at[source],
+            stat_send.at[source],
+            stat_recv.at[source],
+            chip_device(source, core),
+        )
+
+    each_peer(lambda peer: stat_copy(peer).start())
+    each_source(lambda source: stat_arrival(source).wait_recv())
+
+    row_max = all_stats[0, 0:1, :]
+    for index in range(1, chips):
+        row_max = jnp.maximum(row_max, all_stats[index, 0:1, :])
+    exp_total = zero_row
+    target_score = zero_row
+    for index in range(chips):
+        exp_total = exp_total + jnp.exp(all_stats[index, 0:1, :] - row_max)
+        target_score = target_score + all_stats[index, 1:2, :]
+    log_total = row_max + jnp.log(exp_total)
+
+    losses = jnp.broadcast_to(log_total - target_score, (rows, positions))
+    row_index = lax.broadcasted_iota(jnp.int32, (rows, positions), 0)
+    row_place = lax.broadcasted_iota(jnp.int32, (rows, positions), 1)
+    own_losses = jnp.sum(
+        jnp.where(row_place == row_index + own_block * rows, losses, 0.0), axis=1, keepdims=True
+    )
+    cell_row = lax.broadcasted_iota(jnp.int32, (rows, lanes), 0)
+    cell_lane = lax.broadcasted_iota(jnp.int32, (rows, lanes), 1)
+    loss_row = jnp.sum(
+        jnp.where(cell_row == cell_lane, jnp.broadcast_to(own_losses, (rows, lanes)), 0.0),
+        axis=0,
+        keepdims=True,
+    )
+    loss_ref[...] = loss_row[:, :rows]
+
+    grad_t[...] = jnp.zeros_like(grad_t)
+
+    def backward_states(index, carried):
+        base = pl.multiple_of(index * chunk, chunk)
+        factor = weight * jnp.exp(chunk_max[index] - log_total)
+        item_index = lax.broadcasted_iota(jnp.int32, (chunk, positions), 0)
+        matched = item_index == local_target - base
+        part = probs[pl.ds(base, chunk), :] * factor - jnp.where(
+            matched, jnp.broadcast_to(weight, (chunk, positions)), 0.0
+        )
+        part = part.astype(jnp.bfloat16)
+        signal[pl.ds(base, chunk), :] = part
+        grad_t[...] += jnp.dot(
+            items_t[:, pl.ds(base, chunk)], part, preferred_element_type=jnp.float32
+        )
+        return carried
+
+    lax.fori_loop(0, chunk_count, backward_states, 0)
+
+    turned = grad_t[...].T
+    for group in range(group_size):
+        for rank in range(item_size):
+            start = (group * item_size + rank) * rows
+            grads[rank % 2, group * chips_per_group + rank // 2] = turned[start : start + rows, :]
+
+    grad_mate = remote(
+        grads.at[1 - core], mate_grads, grad_mate_sems.at[0], grad_mate_sems.at[1], mate
+    )
+    grad_mate.start()
+
+    def out_copy(index):
+        span = pl.ds(pl.multiple_of(index * chunk, chunk), chunk)
+        return pltpu.make_async_copy(stage.at[span], tgrad_ref.at[span], out_sems.at[index])
+
+    def backward_items(index, carried):
+        base = pl.multiple_of(index * chunk, chunk)
+        stage[pl.ds(base, chunk), :] = jnp.dot(
+            signal[pl.ds(base, chunk), :], states[...], preferred_element_type=jnp.float32
+        ).astype(jnp.bfloat16)
+        out_copy(index).start()
+        return carried
+
+    early = chunk_count // 2
+    lax.fori_loop(0, early, backward_items, 0)
+
+    grad_mate.wait()
+    send_grads[...] = (grads[core] + mate_grads[...]).astype(send_grads.dtype)
+
+    def grad_copy(peer):
+        return remote(
+            send_grads.at[peer],
+            recv_grads.at[chip],
+            grad_send.at[peer],
+            grad_recv.at[chip],
+            chip_device(peer, core),
+        )
+
+    def grad_arrival(source):
+        return remote(
+            send_grads.at[source],
+            recv_grads.at[source],
+            grad_send.at[source],
+            grad_recv.at[source],
+            chip_device(source, core),
+        )
+
+    each_peer(lambda peer: grad_copy(peer).start())
+    recv_grads[chip] = send_grads[chip]
+
+    lax.fori_loop(early, chunk_count, backward_items, 0)
+
+    each_source(lambda source: grad_arrival(source).wait_recv())
+    total = recv_grads[0].astype(jnp.float32)
+    for index in range(1, chips):
+        total = total + recv_grads[index].astype(jnp.float32)
+    hgrad_ref[...] = total.astype(jnp.bfloat16)
+
+    relay_copy(chip).wait_send()
+
+    def finish(peer):
+        gather_copy(peer).wait_send()
+        relay_copy(peer).wait_send()
+        stat_copy(peer).wait_send()
+        grad_copy(peer).wait_send()
+
+    each_peer(finish)
+
+    def drain(index, carried):
+        out_copy(index).wait()
+        return carried
+
+    lax.fori_loop(0, chunk_count, drain, 0)
+
+
+def fused(item_size, group_size, chunk, wire, hidden, item_table, targets, lengths):
+    rows, width = hidden.shape
+    half = item_table.shape[0] // group_size
+    positions = rows * item_size * group_size
+    chips = item_size * group_size // 2
+    chunk_count = half // chunk
+    padded = rows + 8
+    vmem = pl.BlockSpec(memory_space=pltpu.VMEM)
+    dma = pltpu.SemaphoreType.DMA
+    f32, bf16 = jnp.float32, jnp.bfloat16
+    loss, hgrad, tgrad = pl.pallas_call(
+        functools.partial(fused_kernel, item_size, group_size, chunk),
+        out_shape=(
+            jax.ShapeDtypeStruct((1, rows), f32),
+            jax.ShapeDtypeStruct((rows, width), bf16),
+            jax.ShapeDtypeStruct((half, width), bf16),
+        ),
+        in_specs=[
+            vmem,
+            vmem,
+            pl.BlockSpec(memory_space=pltpu.SMEM),
+            pl.BlockSpec(memory_space=pl.ANY),
+        ],
+        out_specs=(vmem, vmem, pl.BlockSpec(memory_space=pl.ANY)),
+        scratch_shapes=[
+            pltpu.VMEM((8, width), jnp.int32),
+            pltpu.VMEM((2 * chips, padded, width), bf16),
+            pltpu.VMEM((positions, width), bf16),
+            pltpu.VMEM((half, width), bf16),
+            pltpu.VMEM((width, half), bf16),
+            pltpu.VMEM((half, positions), f32),
+            pltpu.VMEM((half, positions), bf16),
+            pltpu.VMEM((chunk_count, 1, positions), f32),
+            pltpu.VMEM((2, positions), f32),
+            pltpu.VMEM((2, positions), f32),
+            pltpu.VMEM((chips, 2, positions), f32),
+            pltpu.VMEM((width, positions), f32),
+            pltpu.VMEM((2, chips, rows, width), f32),
+            pltpu.VMEM((chips, rows, width), f32),
+            pltpu.VMEM((chips, rows, width), wire),
+            pltpu.VMEM((chips, rows, width), wire),
+            pltpu.VMEM((half, width), bf16),
+            dma,
+            dma((chunk_count,)),
+            dma((chips,)),
+            dma((chips,)),
+            dma((chips,)),
+            dma((chips,)),
+            dma((2,)),
+            dma((chips,)),
+            dma((chips,)),
+            dma((2,)),
+            dma((chips,)),
+            dma((chips,)),
+        ],
+        compiler_params=pltpu.CompilerParams(
+            collective_id=0, has_side_effects=True, vmem_limit_bytes=60 * 1024 * 1024
+        ),
+        name="fused_loss",
+    )(hidden, targets.reshape(1, rows), lengths, item_table)
+    return loss.reshape(rows), hgrad, tgrad
+
+
 def solution(mesh):
     in_specs = (P(("grp", "item"), None), P("item", None), P(("grp", "item")), P())
     out_specs = (P(("grp", "item")), P(("grp", "item"), None), P(("item", "grp"), None))
-    return jax.shard_map(local, mesh=mesh, in_specs=in_specs, out_specs=out_specs, check_vma=False)
+    item_size, group_size = mesh.shape["item"], mesh.shape["grp"]
+
+    def body(hidden, item_table, targets, lengths):
+        rows, width = hidden.shape
+        half = item_table.shape[0] // group_size
+        chunk = min(512, half)
+        fits = (
+            rows % 8 == 0
+            and rows <= 128
+            and width % 128 == 0
+            and item_size % 2 == 0
+            and half * group_size == item_table.shape[0]
+            and half % chunk == 0
+            and chunk % 128 == 0
+            and (rows * item_size * group_size) % 128 == 0
+            and item_size * item_table.shape[0] <= 1 << 24
+        )
+        if fits:
+            return fused(
+                item_size, group_size, chunk, jnp.float32, hidden, item_table, targets, lengths
+            )
+        return local(hidden, item_table, targets, lengths)
+
+    return jax.shard_map(body, mesh=mesh, in_specs=in_specs, out_specs=out_specs, check_vma=False)

time: 237 us -> 54.2 us (0.23)
  the two profiles are of different devices: /device:TPU:1 before, /device:TPU:0 now
where the time goes in v1:
time: 54.2 us; the launch traced here: 53.9 us
  Pallas kernels  47.8 us (88%)
  local copies, waits for them, and re-layouts  5.47 us (10%)
  between operations  0.64 us (1%)
    pallas_call x1, Pallas kernels, fused(): pl.pallas_call(functools.partial(fused_kernel, item_size, group_size, chu...  47.8 us
    unnamed x3, local copies, waits for them, and re-layouts  5.47 us

profile of v1, /device:TPU:0, one launch (start us, length us, event | category | flops | bytes accessed | tf_op | source)
XLA Modules:
  0.0 53.9 jit_solution(17488126445751098889)
XLA Ops:
  0.6 47.8 %fused_loss.1 = (f32[1,24]{1,0:T(1,128)}, bf16[24,256]{1,0:T(8,128)(2,1)}, bf16[4096,256]{1,0:T(8,128)(2,1)}) custom-call(bf16[24,256]{1,0:T(8,128)(2,1)} %hidden_ref.1, s32[1,24]{1,0:T(1,128)} %bitcast.2, s32[2,16]{1,0:T(2,128)} %lengths_ref.1, bf16[8192,256]{1,0:T(8,128)(2,1)} %table_ref.1), custom_call_target="tpu_custom_call" | custom-call | tf_op jit(solution)/shard_map/fused_loss/pallas_call | solution.py:531
  48.4 1.1 %copy.10 = f32[24]{0:T(128)} copy(f32[24]{0:T(128)} %bitcast.3) | data formatting | bytes 192
  49.5 1.3 %copy.11 = bf16[24,256]{1,0:T(8,128)(2,1)} copy(bf16[24,256]{1,0:T(8,128)(2,1)} %get-tuple-element.13) | data formatting | bytes 24576
  50.8 3.0 %copy.12 = bf16[4096,256]{1,0:T(8,128)(2,1)} copy(bf16[4096,256]{1,0:T(8,128)(2,1)} %get-tuple-element.14) | data formatting | bytes 4194304

commit v2 on v1

v2 whole, which is shorter than its diff:
```python
import functools
import jax
import jax.numpy as jnp
from jax import lax
from jax.experimental import pallas as pl
from jax.experimental.pallas import tpu as pltpu
from jax.sharding import PartitionSpec as P


def block_width():
    return 2048


def weights_for(lengths, group_index, group_rows):
    seq_count = lengths.shape[1]
    own_lengths = lax.dynamic_index_in_dim(lengths, group_index, 0, keepdims=False)
    seq_ends = jnp.cumsum(own_lengths)
    starts = seq_ends - own_lengths
    places = jnp.arange(group_rows, dtype=jnp.int32)
    inside = (places[:, None] >= starts[None, :]) & (places[:, None] < seq_ends[None, :])
    row_length = jnp.sum(
        jnp.where(inside, own_lengths[None, :].astype(jnp.float32), jnp.float32(0.0)), axis=1
    )
    return group_rows / seq_count / row_length


def split_blocks(item_table, first_item, block_size):
    block_count = item_table.shape[0] // block_size
    blocks = item_table.reshape(block_count, block_size, item_table.shape[1])
    block_starts = first_item + block_size * jnp.arange(block_count, dtype=jnp.int32)
    return (blocks, block_starts)


def partial_stats(states, target_ids, item_table, first_item, block_size):
    blocks, block_starts = split_blocks(item_table, first_item, block_size)
    row_count = states.shape[0]

    def partial_visit(carried, block_pair):
        highest, running, picked = carried
        item_block, block_start = block_pair
        scores = jnp.einsum("rd,id->ri", states, item_block, preferred_element_type=jnp.float32)
        new_max = jnp.maximum(highest, jnp.max(scores, axis=1))
        running = running * jnp.exp(highest - new_max) + jnp.sum(
            jnp.exp(scores - new_max[:, None]), axis=1
        )
        columns = block_start + jnp.arange(block_size, dtype=jnp.int32)
        matched = target_ids[:, None] == columns[None, :]
        picked = picked + jnp.sum(jnp.where(matched, scores, jnp.float32(0.0)), axis=1)
        return ((new_max, running, picked), None)

    start_stats = (
        jnp.full((row_count,), -jnp.inf, dtype=jnp.float32),
        jnp.zeros((row_count,), jnp.float32),
        jnp.zeros((row_count,), jnp.float32),
    )
    final_stats, unused = lax.scan(partial_visit, start_stats, (blocks, block_starts))
    return final_stats


def backward(states, target_ids, item_table, first_item, block_size, log_total, row_weight):
    blocks, block_starts = split_blocks(item_table, first_item, block_size)

    def backward_visit(state_grad, block_pair):
        item_block, block_start = block_pair
        scores = jnp.einsum("rd,id->ri", states, item_block, preferred_element_type=jnp.float32)
        columns = block_start + jnp.arange(block_size, dtype=jnp.int32)
        matched = (target_ids[:, None] == columns[None, :]).astype(jnp.float32)
        signal = (row_weight[:, None] * (jnp.exp(scores - log_total[:, None]) - matched)).astype(
            jnp.bfloat16
        )
        state_grad = state_grad + jnp.dot(signal, item_block, preferred_element_type=jnp.float32)
        item_grad = jnp.einsum("ri,rd->id", signal, states, preferred_element_type=jnp.float32)
        return (state_grad, item_grad)

    start_grad = jnp.zeros((states.shape[0], states.shape[1]), jnp.float32)
    state_grad, item_grads = lax.scan(backward_visit, start_grad, (blocks, block_starts))
    return (state_grad, item_grads.reshape(item_table.shape[0], item_table.shape[1]))


def local(hidden, item_table, targets, lengths):
    rows_local = hidden.shape[0]
    items_local = item_table.shape[0]
    block_size = block_width()
    item_rank = lax.axis_index("item")
    group_rank = lax.axis_index("grp")
    first_item = item_rank * items_local
    group_states, group_targets = (
        lax.all_gather(hidden, "item", axis=0, tiled=True),
        lax.all_gather(targets, "item", axis=0, tiled=True),
    )
    group_rows = group_states.shape[0]
    states, target_ids = (
        lax.all_gather(group_states, "grp", axis=0, tiled=True),
        lax.all_gather(group_targets, "grp", axis=0, tiled=True),
    )
    row_weight = jnp.concatenate(
        [weights_for(lengths, member, group_rows) for member in range(lengths.shape[0])]
    )
    own_start = group_rank * group_rows + item_rank * rows_local
    highest, running, picked = partial_stats(states, target_ids, item_table, first_item, block_size)
    row_max = lax.pmax(highest, "item")
    exp_total, target_score = lax.psum((running * jnp.exp(highest - row_max), picked), "item")
    log_total = row_max + jnp.log(exp_total)
    losses = log_total - target_score
    row_loss = lax.dynamic_slice_in_dim(losses, own_start, rows_local)
    half_items = items_local // 2
    own_items = lax.dynamic_slice_in_dim(item_table, group_rank * half_items, half_items)
    state_grad, table_grad = backward(
        states,
        target_ids,
        own_items,
        first_item + group_rank * half_items,
        block_width(),
        log_total,
        row_weight,
    )
    group_grad = lax.psum_scatter(state_grad, "grp", scatter_dimension=0, tiled=True)
    hidden_grad = lax.psum_scatter(group_grad, "item", scatter_dimension=0, tiled=True)
    return (row_loss, hidden_grad.astype(jnp.bfloat16), table_grad.astype(jnp.bfloat16))


def fused_kernel(
    item_size,
    group_size,
    near_size,
    chunk,
    hidden_ref,
    targets_ref,
    lengths_ref,
    table_ref,
    loss_ref,
    hgrad_ref,
    tgrad_ref,
    target_pad,
    gathered,
    states,
    items,
    items_t,
    probs,
    signal,
    chunk_max,
    own_stats,
    mate_stats,
    all_stats,
    grad_t,
    grads,
    mate_grads,
    send_grads,
    wire_grads,
    recv_grads,
    stage,
    items_sem,
    out_sems,
    gather_send,
    gather_recv,
    relay_send,
    relay_recv,
    stat_mate_send,
    stat_mate_recv,
    stat_send,
    stat_recv,
    grad_mate_sems,
    grad_send,
    grad_recv,
):
    rows, width = hidden_ref.shape
    half = items.shape[0]
    chunk_count = half // chunk
    padded = gathered.shape[2]
    slots = states.shape[1]
    positions = 2 * slots
    chips_per_group = item_size // 2
    chips = chips_per_group * group_size
    far_size = chips_per_group // near_size
    group_rows = rows * item_size
    lanes = 128

    item_rank = lax.axis_index("item")
    group_rank = lax.axis_index("grp")
    core = lax.rem(item_rank, 2)
    in_group = item_rank // 2
    chip = group_rank * chips_per_group + in_group
    near = lax.rem(in_group, near_size)
    far = in_group // near_size
    first_item = (item_rank * group_size + group_rank) * half

    def chip_device(which):
        return {
            "item": 2 * lax.rem(which, chips_per_group) + core,
            "grp": which // chips_per_group,
        }

    mate = {"item": 2 * in_group + 1 - core, "grp": group_rank}

    def remote(src, dst, send_sem, recv_sem, device):
        return pltpu.make_async_remote_copy(
            src_ref=src,
            dst_ref=dst,
            send_sem=send_sem,
            recv_sem=recv_sem,
            device_id=device,
            device_id_type=pl.DeviceIdType.MESH,
        )

    def each_peer(body):
        def step(offset, carried):
            body(lax.rem(chip + offset, chips))
            return carried

        lax.fori_loop(1, chips, step, 0)

    def flipped(offset):
        place = far
        for bit in range(offset.bit_length()):
            size = 1 << bit
            if offset & size:
                place = place + size - 2 * size * lax.rem(far // size, 2)
        return place

    far_places = [flipped(offset) for offset in range(far_size)]
    columns = [
        (lax.rem(near + step_near, near_size), lax.rem(group_rank + step_group, group_size))
        for step_near in range(near_size)
        for step_group in range(group_size)
    ]

    def chip_at(column, place):
        return column[1] * chips_per_group + place * near_size + column[0]

    far_chips = [chip_at(columns[0], place) for place in far_places[1:]]
    near_chips = [chip_at(column, far) for column in columns[1:]]

    items_copy = pltpu.make_async_copy(
        table_ref.at[pl.ds(pl.multiple_of(group_rank * half, chunk), half)], items, items_sem
    )
    items_copy.start()

    barrier = pltpu.get_barrier_semaphore()
    greeted = [mate] + [chip_device(peer) for peer in far_chips + near_chips]
    for device in greeted:
        pl.semaphore_signal(
            barrier, inc=1, device_id=device, device_id_type=pl.DeviceIdType.MESH
        )

    target_pad[...] = jnp.zeros_like(target_pad)
    target_pad[0:1, 0:rows] = targets_ref[...]
    wide_targets = jnp.broadcast_to(target_pad[0:1, :], (8, width))
    digit_row = lax.broadcasted_iota(jnp.int32, (8, width), 0)
    digits = jnp.where(
        digit_row == 0,
        wide_targets & 255,
        jnp.where(
            digit_row == 1,
            (wide_targets >> 8) & 255,
            jnp.where(digit_row == 2, (wide_targets >> 16) & 255, 0),
        ),
    ).astype(jnp.float32)
    gathered[core, chip] = jnp.concatenate(
        [hidden_ref[...].astype(jnp.float32), digits], axis=0
    ).astype(jnp.bfloat16)

    pl.semaphore_wait(barrier, len(greeted))

    def gather_copy(source, lane, peer):
        block = gathered.at[core, source]
        return remote(
            block, block, gather_send.at[lane], gather_recv.at[source], chip_device(peer)
        )

    def relay_copy(source):
        block = gathered.at[core, source]
        return remote(block, block, relay_send.at[source], relay_recv.at[source], mate)

    def relay_arrival(source):
        block = gathered.at[1 - core, source]
        return remote(block, block, relay_send.at[source], relay_recv.at[source], mate)

    sent = []

    def send_on(source, peers):
        for peer in peers:
            copy = gather_copy(source, len(sent), peer)
            copy.start()
            sent.append(copy)

    send_on(chip, far_chips)
    send_on(chip, near_chips)
    relay_copy(chip).start()

    slot_index = lax.broadcasted_iota(jnp.int32, (1, positions), 1)
    slot_block = slot_index // rows
    slot_chip = lax.rem(slot_block, chips)
    places = (
        (slot_chip // chips_per_group) * item_size
        + 2 * lax.rem(slot_chip, chips_per_group)
        + slot_block // chips
    ) * rows + lax.rem(slot_index, rows)
    row_length = jnp.zeros((1, positions), jnp.float32)
    for member in range(group_size):
        start = member * group_rows
        for seq in range(lengths_ref.shape[1]):
            length = lengths_ref[member, seq]
            inside = (places >= start) & (places < start + length)
            row_length = jnp.where(inside, length.astype(jnp.float32), row_length)
            start = start + length
    weight = (group_rows / lengths_ref.shape[1]) / row_length

    items_copy.wait()
    for index in range(chunk_count):
        span = pl.ds(index * chunk, chunk)
        items_t[:, span] = items[span, :].astype(jnp.float32).T.astype(jnp.bfloat16)

    for source in far_chips:
        gather_copy(source, 0, source).wait_recv()
        send_on(source, near_chips)
        relay_copy(source).start()
    others = [chip_at(column, place) for place in far_places for column in columns[1:]]
    for source in others:
        gather_copy(source, 0, source).wait_recv()
        relay_copy(source).start()
    all_chips = [chip] + far_chips + others
    for source in all_chips:
        relay_arrival(source).wait_recv()

    everything = gathered[...].reshape(2 * chips, padded, width).astype(jnp.float32)
    states[...] = (
        everything[:, :rows, :].reshape(2, slots, width).astype(jnp.bfloat16)
    )
    code = everything[:, rows:padded, :lanes]
    code_rows = code.shape[0] * code.shape[1]
    code = code.reshape(code_rows, lanes).astype(jnp.bfloat16)
    lane_index = lax.broadcasted_iota(jnp.int32, (lanes, positions), 0)
    place_index = lax.broadcasted_iota(jnp.int32, (lanes, positions), 1)
    spread = (lax.rem(place_index, rows) == lane_index).astype(jnp.float32).astype(jnp.bfloat16)
    coded = jnp.dot(code, spread, preferred_element_type=jnp.float32)
    code_index = lax.broadcasted_iota(jnp.int32, (code_rows, positions), 0)
    code_place = lax.broadcasted_iota(jnp.int32, (code_rows, positions), 1)
    digit = lax.rem(code_index, 8)
    scale = jnp.where(
        digit == 0,
        jnp.float32(1.0),
        jnp.where(
            digit == 1,
            jnp.float32(256.0),
            jnp.where(digit == 2, jnp.float32(65536.0), jnp.float32(0.0)),
        ),
    )
    target_ids = jnp.sum(
        jnp.where(code_index // 8 == code_place // rows, coded * scale, 0.0),
        axis=0,
        keepdims=True,
    ).astype(jnp.int32)
    local_target = target_ids - first_item

    def part_of(row, part):
        return row[:, part * slots : (part + 1) * slots]

    def forward(part):
        wanted = part_of(local_target, part)

        def visit(index, carried):
            highest, running, picked = carried
            base = pl.multiple_of(index * chunk, chunk)
            scores = lax.dot_general(
                items[pl.ds(base, chunk), :],
                states[part],
                (((1,), (1,)), ((), ())),
                preferred_element_type=jnp.float32,
            )
            top = jnp.max(scores, axis=0, keepdims=True)
            exps = jnp.exp(scores - top)
            probs[part, pl.ds(base, chunk), :] = exps
            chunk_max[part, index] = top
            total = jnp.sum(exps, axis=0, keepdims=True)
            item_index = lax.broadcasted_iota(jnp.int32, (chunk, slots), 0)
            matched = item_index == wanted - base
            picked = picked + jnp.sum(jnp.where(matched, scores, 0.0), axis=0, keepdims=True)
            new_max = jnp.maximum(highest, top)
            running = running * jnp.exp(highest - new_max) + total * jnp.exp(top - new_max)
            return (new_max, running, picked)

        return visit

    zero_row = jnp.zeros((1, slots), jnp.float32)
    start_stats = (jnp.full((1, slots), -jnp.inf, jnp.float32), zero_row, zero_row)

    def log_add(a, b):
        top = jnp.maximum(a, b)
        return top + jnp.log(jnp.exp(a - top) + jnp.exp(b - top))

    def stat_mate(part):
        return remote(
            own_stats.at[part],
            mate_stats.at[part],
            stat_mate_send.at[part],
            stat_mate_recv.at[part],
            mate,
        )

    def stat_copy(part, source, peer):
        block = all_stats.at[part, source]
        return remote(
            block, block, stat_send.at[part, peer], stat_recv.at[part, source], chip_device(peer)
        )

    def share_stats(part, found):
        highest, running, picked = found
        own_stats[part, 0:1, :] = highest + jnp.log(running)
        own_stats[part, 1:2, :] = picked
        stat_mate(part).start()

    def spread_stats(part):
        stat_mate(part).wait()
        all_stats[part, chip] = jnp.concatenate(
            [
                log_add(own_stats[part, 0:1, :], mate_stats[part, 0:1, :]),
                own_stats[part, 1:2, :] + mate_stats[part, 1:2, :],
            ],
            axis=0,
        )
        each_peer(lambda peer: stat_copy(part, chip, peer).start())

    def collect_stats(part):
        each_peer(lambda source: stat_copy(part, source, source).wait_recv())
        row_max = all_stats[part, 0, 0:1, :]
        for index in range(1, chips):
            row_max = jnp.maximum(row_max, all_stats[part, index, 0:1, :])
        exp_total = zero_row
        target_score = zero_row
        for index in range(chips):
            exp_total = exp_total + jnp.exp(all_stats[part, index, 0:1, :] - row_max)
            target_score = target_score + all_stats[part, index, 1:2, :]
        log_total = row_max + jnp.log(exp_total)

        @pl.when(core == part)
        def write_losses():
            losses = jnp.broadcast_to(log_total - target_score, (rows, slots))
            row_index = lax.broadcasted_iota(jnp.int32, (rows, slots), 0)
            row_place = lax.broadcasted_iota(jnp.int32, (rows, slots), 1)
            own_losses = jnp.sum(
                jnp.where(row_place == row_index + chip * rows, losses, 0.0),
                axis=1,
                keepdims=True,
            )
            cell_row = lax.broadcasted_iota(jnp.int32, (rows, lanes), 0)
            cell_lane = lax.broadcasted_iota(jnp.int32, (rows, lanes), 1)
            loss_row = jnp.sum(
                jnp.where(
                    cell_row == cell_lane, jnp.broadcast_to(own_losses, (rows, lanes)), 0.0
                ),
                axis=0,
                keepdims=True,
            )
            loss_ref[...] = loss_row[:, :rows]

        return log_total

    def backward_states(part, log_total):
        wanted = part_of(local_target, part)
        part_weight = part_of(weight, part)
        grad_t[...] = jnp.zeros_like(grad_t)

        def visit(index, carried):
            base = pl.multiple_of(index * chunk, chunk)
            factor = part_weight * jnp.exp(chunk_max[part, index] - log_total)
            item_index = lax.broadcasted_iota(jnp.int32, (chunk, slots), 0)
            matched = item_index == wanted - base
            value = probs[part, pl.ds(base, chunk), :] * factor - jnp.where(
                matched, jnp.broadcast_to(part_weight, (chunk, slots)), 0.0
            )
            value = value.astype(jnp.bfloat16)
            signal[part, pl.ds(base, chunk), :] = value
            grad_t[...] += jnp.dot(
                items_t[:, pl.ds(base, chunk)], value, preferred_element_type=jnp.float32
            )
            return carried

        return visit

    grad_mate = remote(grads, mate_grads, grad_mate_sems.at[0], grad_mate_sems.at[1], mate)

    def hand_over(part):
        turned = grad_t[...].T.reshape(chips, rows, width)

        @pl.when(core == part)
        def keep():
            send_grads[...] = turned

        @pl.when(core != part)
        def give():
            grads[...] = turned
            grad_mate.start()

    def grad_copy(source, peer):
        return remote(
            wire_grads.at[peer],
            recv_grads.at[source],
            grad_send.at[peer],
            grad_recv.at[source],
            chip_device(peer),
        )

    def send_out(part):
        @pl.when(core == part)
        def combine():
            grad_mate.wait_recv()
            wire_grads[...] = (send_grads[...] + mate_grads[...]).astype(wire_grads.dtype)
            each_peer(lambda peer: grad_copy(chip, peer).start())
            recv_grads[chip] = wire_grads[chip]

    def out_copy(index):
        span = pl.ds(pl.multiple_of(index * chunk, chunk), chunk)
        return pltpu.make_async_copy(stage.at[span], tgrad_ref.at[span], out_sems.at[index])

    def backward_items(index, carried):
        base = pl.multiple_of(index * chunk, chunk)
        value = jnp.dot(
            signal[0, pl.ds(base, chunk), :], states[0], preferred_element_type=jnp.float32
        ) + jnp.dot(
            signal[1, pl.ds(base, chunk), :], states[1], preferred_element_type=jnp.float32
        )
        stage[pl.ds(base, chunk), :] = value.astype(jnp.bfloat16)
        out_copy(index).start()
        return carried

    early = chunk_count // 2
    share_stats(0, lax.fori_loop(0, chunk_count, forward(0), start_stats))
    found = lax.fori_loop(0, early, forward(1), start_stats)
    spread_stats(0)
    share_stats(1, lax.fori_loop(early, chunk_count, forward(1), found))
    spread_stats(1)
    first_total = collect_stats(0)
    lax.fori_loop(0, chunk_count, backward_states(0, first_total), 0)
    hand_over(0)
    second_total = collect_stats(1)
    visit = backward_states(1, second_total)
    lax.fori_loop(0, early, visit, 0)
    send_out(0)
    lax.fori_loop(early, chunk_count, visit, 0)
    hand_over(1)
    lax.fori_loop(0, early, backward_items, 0)
    send_out(1)
    lax.fori_loop(early, chunk_count, backward_items, 0)

    each_peer(lambda source: grad_copy(source, source).wait_recv())
    total = recv_grads[0].astype(jnp.float32)
    for index in range(1, chips):
        total = total + recv_grads[index].astype(jnp.float32)
    hgrad_ref[...] = total.astype(jnp.bfloat16)

    for copy in sent:
        copy.wait_send()
    for source in all_chips:
        relay_copy(source).wait_send()
    grad_mate.wait_send()

    def finish(peer):
        stat_copy(0, chip, peer).wait_send()
        stat_copy(1, chip, peer).wait_send()
        grad_copy(chip, peer).wait_send()

    each_peer(finish)

    def drain(index, carried):
        out_copy(index).wait()
        return carried

    lax.fori_loop(0, chunk_count, drain, 0)


def fused(item_size, group_size, chunk, wire, hidden, item_table, targets, lengths):
    rows, width = hidden.shape
    half = item_table.shape[0] // group_size
    chips = item_size * group_size // 2
    slots = rows * chips
    chunk_count = half // chunk
    padded = rows + 8
    near_size = 2 if item_size % 4 == 0 else 1
    far_size = item_size // 2 // near_size
    gather_sends = far_size - 1 + far_size * (near_size * group_size - 1)
    vmem = pl.BlockSpec(memory_space=pltpu.VMEM)
    dma = pltpu.SemaphoreType.DMA
    f32, bf16 = jnp.float32, jnp.bfloat16
    loss, hgrad, tgrad = pl.pallas_call(
        functools.partial(fused_kernel, item_size, group_size, near_size, chunk),
        out_shape=(
            jax.ShapeDtypeStruct((1, rows), f32),
            jax.ShapeDtypeStruct((rows, width), bf16),
            jax.ShapeDtypeStruct((half, width), bf16),
        ),
        in_specs=[
            vmem,
            vmem,
            pl.BlockSpec(memory_space=pltpu.SMEM),
            pl.BlockSpec(memory_space=pl.ANY),
        ],
        out_specs=(vmem, vmem, pl.BlockSpec(memory_space=pl.ANY)),
        scratch_shapes=[
            pltpu.VMEM((8, width), jnp.int32),
            pltpu.VMEM((2, chips, padded, width), bf16),
            pltpu.VMEM((2, slots, width), bf16),
            pltpu.VMEM((half, width), bf16),
            pltpu.VMEM((width, half), bf16),
            pltpu.VMEM((2, half, slots), f32),
            pltpu.VMEM((2, half, slots), bf16),
            pltpu.VMEM((2, chunk_count, 1, slots), f32),
            pltpu.VMEM((2, 2, slots), f32),
            pltpu.VMEM((2, 2, slots), f32),
            pltpu.VMEM((2, chips, 2, slots), f32),
            pltpu.VMEM((width, slots), f32),
            pltpu.VMEM((chips, rows, width), f32),
            pltpu.VMEM((chips, rows, width), f32),
            pltpu.VMEM((chips, rows, width), f32),
            pltpu.VMEM((chips, rows, width), wire),
            pltpu.VMEM((chips, rows, width), wire),
            pltpu.VMEM((half, width), bf16),
            dma,
            dma((chunk_count,)),
            dma((gather_sends,)),
            dma((chips,)),
            dma((chips,)),
            dma((chips,)),
            dma((2,)),
            dma((2,)),
            dma((2, chips)),
            dma((2, chips)),
            dma((2,)),
            dma((chips,)),
            dma((chips,)),
        ],
        compiler_params=pltpu.CompilerParams(
            collective_id=0, has_side_effects=True, vmem_limit_bytes=60 * 1024 * 1024
        ),
        name="fused_loss",
    )(hidden, targets.reshape(1, rows), lengths, item_table)
    return loss.reshape(rows), hgrad, tgrad


def solution(mesh):
    in_specs = (P(("grp", "item"), None), P("item", None), P(("grp", "item")), P())
    out_specs = (P(("grp", "item")), P(("grp", "item"), None), P(("item", "grp"), None))
    item_size, group_size = mesh.shape["item"], mesh.shape["grp"]

    def body(hidden, item_table, targets, lengths):
        rows, width = hidden.shape
        half = item_table.shape[0] // group_size
        chunk = min(512, half)
        fits = (
            rows % 8 == 0
            and rows <= 128
            and width % 128 == 0
            and item_size % 2 == 0
            and half * group_size == item_table.shape[0]
            and half % chunk == 0
            and chunk % 128 == 0
            and (rows * item_size * group_size) % 256 == 0
            and (item_size & (item_size - 1)) == 0
            and item_size * item_table.shape[0] <= 1 << 24
        )
        if fits:
            return fused(
                item_size, group_size, chunk, jnp.bfloat16, hidden, item_table, targets, lengths
            )
        return local(hidden, item_table, targets, lengths)

    return jax.shard_map(body, mesh=mesh, in_specs=in_specs, out_specs=out_specs, check_vma=False)
```

time: 54.2 us -> 46.7 us (0.86)
  the two profiles are of different devices: /device:TPU:0 before, /device:TPU:1 now
where the time goes in v2:
time: 46.7 us; the launch traced here: 46.3 us
  Pallas kernels  40.2 us (86%)
  local copies, waits for them, and re-layouts  5.47 us (12%)
  between operations  0.64 us (1%)
    pallas_call x1, Pallas kernels, fused(): pl.pallas_call(functools.partial(fused_kernel, item_size, group_size, nea...  40.2 us
    unnamed x3, local copies, waits for them, and re-layouts  5.47 us

profile of v2, /device:TPU:1, one launch (start us, length us, event | category | flops | bytes accessed | tf_op | source)
XLA Modules:
  0.0 46.3 jit_solution(14267665076360877359)
XLA Ops:
  0.6 40.2 %fused_loss.1 = (f32[1,24]{1,0:T(1,128)}, bf16[24,256]{1,0:T(8,128)(2,1)}, bf16[4096,256]{1,0:T(8,128)(2,1)}) custom-call(bf16[24,256]{1,0:T(8,128)(2,1)} %hidden_ref.1, s32[1,24]{1,0:T(1,128)} %bitcast.2, s32[2,16]{1,0:T(2,128)} %lengths_ref.1, bf16[8192,256]{1,0:T(8,128)(2,1)} %table_ref.1), custom_call_target="tpu_custom_call" | custom-call | tf_op jit(solution)/shard_map/fused_loss/pallas_call | solution.py:584
  40.9 1.1 %copy.10 = f32[24]{0:T(128)} copy(f32[24]{0:T(128)} %bitcast.3) | data formatting | bytes 192
  42.0 1.3 %copy.11 = bf16[24,256]{1,0:T(8,128)(2,1)} copy(bf16[24,256]{1,0:T(8,128)(2,1)} %get-tuple-element.13) | data formatting | bytes 24576
  43.3 3.0 %copy.12 = bf16[4096,256]{1,0:T(8,128)(2,1)} copy(bf16[4096,256]{1,0:T(8,128)(2,1)} %get-tuple-element.14) | data formatting | bytes 4194304

commit v3 on v2

--- a/solution.py
+++ b/solution.py
@@ -135,14 +135,13 @@
     gathered,
     states,
     items,
-    items_t,
     probs,
     signal,
     chunk_max,
     own_stats,
     mate_stats,
     all_stats,
-    grad_t,
+    grad_rows,
     grads,
     mate_grads,
     send_grads,
@@ -167,8 +166,8 @@
     half = items.shape[0]
     chunk_count = half // chunk
     padded = gathered.shape[2]
-    slots = states.shape[1]
-    positions = 2 * slots
+    positions = states.shape[0]
+    slots = positions // 2
     chips_per_group = item_size // 2
     chips = chips_per_group * group_size
     far_size = chips_per_group // near_size
@@ -289,12 +288,13 @@
 
     slot_index = lax.broadcasted_iota(jnp.int32, (1, positions), 1)
     slot_block = slot_index // rows
+    slot_row = slot_index - slot_block * rows
     slot_chip = lax.rem(slot_block, chips)
     places = (
         (slot_chip // chips_per_group) * item_size
         + 2 * lax.rem(slot_chip, chips_per_group)
         + slot_block // chips
-    ) * rows + lax.rem(slot_index, rows)
+    ) * rows + slot_row
     row_length = jnp.zeros((1, positions), jnp.float32)
     for member in range(group_size):
         start = member * group_rows
@@ -305,10 +305,10 @@
             start = start + length
     weight = (group_rows / lengths_ref.shape[1]) / row_length
 
+    lane_index = lax.broadcasted_iota(jnp.int32, (lanes, positions), 0)
+    spread = (slot_row == lane_index).astype(jnp.float32).astype(jnp.bfloat16)
+
     items_copy.wait()
-    for index in range(chunk_count):
-        span = pl.ds(index * chunk, chunk)
-        items_t[:, span] = items[span, :].astype(jnp.float32).T.astype(jnp.bfloat16)
 
     for source in far_chips:
         gather_copy(source, 0, source).wait_recv()
@@ -323,32 +323,18 @@
         relay_arrival(source).wait_recv()
 
     everything = gathered[...].reshape(2 * chips, padded, width).astype(jnp.float32)
-    states[...] = (
-        everything[:, :rows, :].reshape(2, slots, width).astype(jnp.bfloat16)
-    )
+    states[...] = everything[:, :rows, :].reshape(positions, width).astype(jnp.bfloat16)
     code = everything[:, rows:padded, :lanes]
     code_rows = code.shape[0] * code.shape[1]
     code = code.reshape(code_rows, lanes).astype(jnp.bfloat16)
-    lane_index = lax.broadcasted_iota(jnp.int32, (lanes, positions), 0)
-    place_index = lax.broadcasted_iota(jnp.int32, (lanes, positions), 1)
-    spread = (lax.rem(place_index, rows) == lane_index).astype(jnp.float32).astype(jnp.bfloat16)
     coded = jnp.dot(code, spread, preferred_element_type=jnp.float32)
     code_index = lax.broadcasted_iota(jnp.int32, (code_rows, positions), 0)
-    code_place = lax.broadcasted_iota(jnp.int32, (code_rows, positions), 1)
-    digit = lax.rem(code_index, 8)
-    scale = jnp.where(
-        digit == 0,
-        jnp.float32(1.0),
-        jnp.where(
-            digit == 1,
-            jnp.float32(256.0),
-            jnp.where(digit == 2, jnp.float32(65536.0), jnp.float32(0.0)),
-        ),
-    )
-    target_ids = jnp.sum(
-        jnp.where(code_index // 8 == code_place // rows, coded * scale, 0.0),
+    by_digit = jnp.sum(
+        jnp.where(code_index >> 3 == slot_block, coded, 0.0).reshape(2 * chips, 8, positions),
         axis=0,
-        keepdims=True,
+    )
+    target_ids = (
+        by_digit[0:1, :] + 256.0 * by_digit[1:2, :] + 65536.0 * by_digit[2:3, :]
     ).astype(jnp.int32)
     local_target = target_ids - first_item
 
@@ -363,7 +349,7 @@
             base = pl.multiple_of(index * chunk, chunk)
             scores = lax.dot_general(
                 items[pl.ds(base, chunk), :],
-                states[part],
+                states[part * slots : (part + 1) * slots, :],
                 (((1,), (1,)), ((), ())),
                 preferred_element_type=jnp.float32,
             )
@@ -458,7 +444,7 @@
     def backward_states(part, log_total):
         wanted = part_of(local_target, part)
         part_weight = part_of(weight, part)
-        grad_t[...] = jnp.zeros_like(grad_t)
+        grad_rows[...] = jnp.zeros_like(grad_rows)
 
         def visit(index, carried):
             base = pl.multiple_of(index * chunk, chunk)
@@ -469,9 +455,12 @@
                 matched, jnp.broadcast_to(part_weight, (chunk, slots)), 0.0
             )
             value = value.astype(jnp.bfloat16)
-            signal[part, pl.ds(base, chunk), :] = value
-            grad_t[...] += jnp.dot(
-                items_t[:, pl.ds(base, chunk)], value, preferred_element_type=jnp.float32
+            signal[pl.ds(base, chunk), part * slots : (part + 1) * slots] = value
+            grad_rows[...] += lax.dot_general(
+                value,
+                items[pl.ds(base, chunk), :],
+                (((0,), (0,)), ((), ())),
+                preferred_element_type=jnp.float32,
             )
             return carried
 
@@ -480,7 +469,7 @@
     grad_mate = remote(grads, mate_grads, grad_mate_sems.at[0], grad_mate_sems.at[1], mate)
 
     def hand_over(part):
-        turned = grad_t[...].T.reshape(chips, rows, width)
+        turned = grad_rows[...].reshape(chips, rows, width)
 
         @pl.when(core == part)
         def keep():
@@ -515,32 +504,30 @@
     def backward_items(index, carried):
         base = pl.multiple_of(index * chunk, chunk)
         value = jnp.dot(
-            signal[0, pl.ds(base, chunk), :], states[0], preferred_element_type=jnp.float32
-        ) + jnp.dot(
-            signal[1, pl.ds(base, chunk), :], states[1], preferred_element_type=jnp.float32
+            signal[pl.ds(base, chunk), :], states[...], preferred_element_type=jnp.float32
         )
         stage[pl.ds(base, chunk), :] = value.astype(jnp.bfloat16)
         out_copy(index).start()
         return carried
 
     early = chunk_count // 2
-    share_stats(0, lax.fori_loop(0, chunk_count, forward(0), start_stats))
-    found = lax.fori_loop(0, early, forward(1), start_stats)
+    share_stats(0, lax.fori_loop(0, chunk_count, forward(0), start_stats, unroll=4))
+    found = lax.fori_loop(0, early, forward(1), start_stats, unroll=4)
     spread_stats(0)
-    share_stats(1, lax.fori_loop(early, chunk_count, forward(1), found))
+    share_stats(1, lax.fori_loop(early, chunk_count, forward(1), found, unroll=4))
     spread_stats(1)
     first_total = collect_stats(0)
-    lax.fori_loop(0, chunk_count, backward_states(0, first_total), 0)
+    lax.fori_loop(0, chunk_count, backward_states(0, first_total), 0, unroll=4)
     hand_over(0)
     second_total = collect_stats(1)
     visit = backward_states(1, second_total)
-    lax.fori_loop(0, early, visit, 0)
+    lax.fori_loop(0, early, visit, 0, unroll=4)
     send_out(0)
-    lax.fori_loop(early, chunk_count, visit, 0)
+    lax.fori_loop(early, chunk_count, visit, 0, unroll=4)
     hand_over(1)
-    lax.fori_loop(0, early, backward_items, 0)
+    lax.fori_loop(0, early, backward_items, 0, unroll=4)
     send_out(1)
-    lax.fori_loop(early, chunk_count, backward_items, 0)
+    lax.fori_loop(early, chunk_count, backward_items, 0, unroll=4)
 
     each_peer(lambda source: grad_copy(source, source).wait_recv())
     total = recv_grads[0].astype(jnp.float32)
@@ -566,6 +553,50 @@
         return carried
 
     lax.fori_loop(0, chunk_count, drain, 0)
+
+
+def hand_out_kernel(loss_in, hgrad_in, tgrad_in, loss_out, hgrad_out, tgrad_out, held, sems, outs):
+    count = held.shape[0]
+    block = held.shape[1]
+
+    def span(index):
+        return pl.ds(index * block, block)
+
+    loads = [
+        pltpu.make_async_copy(tgrad_in.at[span(index)], held.at[index], sems.at[index])
+        for index in range(count)
+    ]
+    stores = [
+        pltpu.make_async_copy(held.at[index], tgrad_out.at[span(index)], outs.at[index])
+        for index in range(count)
+    ]
+    for load in loads:
+        load.start()
+    loss_out[...] = loss_in[...]
+    hgrad_out[...] = hgrad_in[...]
+    for load, store in zip(loads, stores):
+        load.wait()
+        store.start()
+    for store in stores:
+        store.wait()
+
+
+def hand_out(chunk, loss, hgrad, tgrad):
+    vmem = pl.BlockSpec(memory_space=pltpu.VMEM)
+    whole = pl.BlockSpec(memory_space=pl.ANY)
+    count = tgrad.shape[0] // chunk
+    return pl.pallas_call(
+        hand_out_kernel,
+        out_shape=tuple(jax.ShapeDtypeStruct(x.shape, x.dtype) for x in (loss, hgrad, tgrad)),
+        in_specs=[vmem, vmem, whole],
+        out_specs=(vmem, vmem, whole),
+        scratch_shapes=[
+            pltpu.VMEM((count, chunk, tgrad.shape[1]), tgrad.dtype),
+            pltpu.SemaphoreType.DMA((count,)),
+            pltpu.SemaphoreType.DMA((count,)),
+        ],
+        name="hand_out",
+    )(loss, hgrad, tgrad)
 
 
 def fused(item_size, group_size, chunk, wire, hidden, item_table, targets, lengths):
@@ -581,7 +612,7 @@
     vmem = pl.BlockSpec(memory_space=pltpu.VMEM)
     dma = pltpu.SemaphoreType.DMA
     f32, bf16 = jnp.float32, jnp.bfloat16
-    loss, hgrad, tgrad = pl.pallas_call(
+    results = pl.pallas_call(
         functools.partial(fused_kernel, item_size, group_size, near_size, chunk),
         out_shape=(
             jax.ShapeDtypeStruct((1, rows), f32),
@@ -598,16 +629,15 @@
         scratch_shapes=[
             pltpu.VMEM((8, width), jnp.int32),
             pltpu.VMEM((2, chips, padded, width), bf16),
-            pltpu.VMEM((2, slots, width), bf16),
+            pltpu.VMEM((2 * slots, width), bf16),
             pltpu.VMEM((half, width), bf16),
-            pltpu.VMEM((width, half), bf16),
             pltpu.VMEM((2, half, slots), f32),
-            pltpu.VMEM((2, half, slots), bf16),
+            pltpu.VMEM((half, 2 * slots), bf16),
             pltpu.VMEM((2, chunk_count, 1, slots), f32),
             pltpu.VMEM((2, 2, slots), f32),
             pltpu.VMEM((2, 2, slots), f32),
             pltpu.VMEM((2, chips, 2, slots), f32),
-            pltpu.VMEM((width, slots), f32),
+            pltpu.VMEM((slots, width), f32),
             pltpu.VMEM((chips, rows, width), f32),
             pltpu.VMEM((chips, rows, width), f32),
             pltpu.VMEM((chips, rows, width), f32),
@@ -633,6 +663,7 @@
         ),
         name="fused_loss",
     )(hidden, targets.reshape(1, rows), lengths, item_table)
+    loss, hgrad, tgrad = hand_out(chunk, *results)
     return loss.reshape(rows), hgrad, tgrad
 
 

time: 46.7 us -> 41.6 us (0.89)
  local copies, waits for them, and re-layouts: 5.47 us -> 0 us
    unnamed x3 -> x0, local copies, waits for them, and re-layouts: 5.47 us -> none
    pallas_call x0 -> x1, Pallas kernels: none -> 3.71 us  [hand_out(): pl.pallas_call(hand_out_kernel, out_shape=tuple((jax.ShapeDtypeStruct(x.s...]
    pallas_call x1, Pallas kernels: 40.2 us -> 36.9 us  [fused(): pl.pallas_call(functools.partial(fused_kernel, item_size, group_size, nea...]
where the time goes in v3:
time: 41.6 us; the launch traced here: 41.2 us
  Pallas kernels  40.6 us (98%)
  between operations  0.64 us (2%)
    pallas_call x1, Pallas kernels, fused(): pl.pallas_call(functools.partial(fused_kernel, item_size, group_size, nea...  36.9 us
    pallas_call x1, Pallas kernels, hand_out(): pl.pallas_call(hand_out_kernel, out_shape=tuple((jax.ShapeDtypeStruct(x.s...  3.71 us

profile of v3, /device:TPU:1, one launch (start us, length us, event | category | flops | bytes accessed | tf_op | source)
XLA Modules:
  0.0 41.2 jit_solution(11769355988160200449)
XLA Ops:
  0.6 36.9 %fused_loss.1 = (f32[1,24]{1,0:T(1,128)}, bf16[24,256]{1,0:T(8,128)(2,1)}, bf16[4096,256]{1,0:T(8,128)(2,1)}) custom-call(bf16[24,256]{1,0:T(8,128)(2,1)} %hidden_ref.1, s32[1,24]{1,0:T(1,128)} %bitcast.2, s32[2,16]{1,0:T(2,128)} %lengths_ref.1, bf16[8192,256]{1,0:T(8,128)(2,1)} %table_ref.1), custom_call_target="tpu_custom_call" | custom-call | tf_op jit(solution)/shard_map/fused_loss/pallas_call | solution.py:615
  37.5 3.7 %hand_out.1 = (f32[1,24]{1,0:T(1,128)}, bf16[24,256]{1,0:T(8,128)(2,1)}, bf16[4096,256]{1,0:T(8,128)(2,1)}) custom-call(f32[1,24]{1,0:T(1,128)} %get-tuple-element.9.loss_in, bf16[24,256]{1,0:T(8,128)(2,1)} %get-tuple-element.10.hgrad_in, bf16[4096,256]{1,0:T(8,128)(2,1)} %get-tuple-element.11.tgrad_in), custom_call_target="tpu_custom_call" | custom-call | tf_op jit(solution)/shard_map/hand_out/pallas_call | solution.py:588
